TPU v7x, 512 devices: a whole 4x8x8 slice. The times are simulated.
512 devices in a mesh: wide: 32 (over z_lo, x, core), narrow: 16 (over z_hi, y).
Axes of the slice: x: 4, y: 8, z: 8 (z_hi: 2, z_lo: 4; z = z_hi * 4 + z_lo), core: 2. Of those that a mesh axis runs over, the one named last changes fastest.
Arguments:
- exposures: bfloat16 [4, 512, 12288], P(None, 'narrow', 'wide'), may hold values from -6 to 6
- basis_kernels: bfloat16 [5, 21, 21], replicated, may hold values from -0.25 to 0.25
- poly_coef: float32 [4, 5, 6], replicated, may hold values from -3 to 3
- exposure_weight: float32 [4], replicated, may hold values from 0.5 to 2
- row_start: int32 [4], replicated, may hold values from 0 to 256, as said below
- row_count: int32 [4], replicated, may hold values from 128 to 512, as said below
- filter_taps: float32 [21], replicated, may hold values from -1.5 to 1.5
Outputs:
- coadded: float32 [512, 12288], P('narrow', 'wide')
- detection: float32 [512, 12288], P('narrow', 'wide')
Inputs may be any that keep to these rules, and one draw needn't show every extreme that they name: Each row_start is a multiple of 32; row_start[0] is 0 and row_start + row_count never exceeds 512. Each row_count is a multiple of 8; exposure 0 covers the whole band.
All inputs are finite; a program needn't handle non-finite values.
Results may differ from a plain program's by a relative error of at most 0.0003.
Values may be sent and summed in bfloat16 or wider, within the bound.
A program may use at most 64 MiB of HBM per device.

v0:
```python
import math
import jax
import jax.numpy as jnp
from jax import lax
from jax.sharding import PartitionSpec as P


def padded(array, sides, width):
    for axis, dim in sides:
        peers, length = (lax.axis_size(axis), array.shape[dim])
        up = [(i, (i + 1) % peers) for i in range(peers - 1)]
        down = [(j, i) for i, j in up]
        last = lax.slice_in_dim(array, length - width, length, axis=dim)
        initial = lax.slice_in_dim(array, 0, width, axis=dim)
        before = lax.ppermute(last, axis, up)
        after = lax.ppermute(initial, axis, down)
        array = jnp.concatenate([before, array, after], axis=dim)
    return array


def respond(window, basis_kernels):
    side = basis_kernels.shape[1]
    kernel_total = basis_kernels.shape[0]
    out_rows = window.shape[0] - (side - 1)
    out_cols = window.shape[1] - (side - 1)
    block = math.gcd(out_cols, 128)
    block_total = out_cols // block
    span = block + side - 1
    shifted = jnp.stack([window[offset : offset + out_rows] for offset in range(side)])
    patches = jnp.stack(
        [shifted[:, :, index * block : index * block + span] for index in range(block_total)]
    )
    lagged = (
        jnp.arange(span, dtype=jnp.int32)[:, None] - jnp.arange(block, dtype=jnp.int32)[None, :]
    )
    onehot = (lagged[None] == jnp.arange(side, dtype=jnp.int32)[:, None, None]).astype(jnp.float32)
    table = jnp.einsum(
        "kab,bco->acko", basis_kernels.astype(jnp.float32), onehot, precision=lax.Precision.HIGHEST
    )
    table = table.astype(jnp.bfloat16).reshape(side, span, kernel_total * block)
    result = jnp.einsum("jarc,acn->jrn", patches, table, preferred_element_type=jnp.float32)
    result = result.reshape(block_total, out_rows, kernel_total, block).transpose(2, 1, 0, 3)
    return result.reshape(kernel_total, out_rows, out_cols)


def on_device(
    exposures, basis_kernels, poly_coef, exposure_weight, row_start, row_count, filter_taps
):
    tile_rows = exposures.shape[1]
    tile_cols = exposures.shape[2]
    band_rows = tile_rows * lax.axis_size("narrow")
    band_cols = tile_cols * lax.axis_size("wide")
    row_base = lax.axis_index("narrow") * tile_rows
    row_index = row_base + jnp.arange(tile_rows, dtype=jnp.int32)
    col_index = lax.axis_index("wide") * tile_cols + jnp.arange(tile_cols, dtype=jnp.int32)
    y_coord = ((2 * row_index + 1).astype(jnp.float32) / band_rows - 1.0)[:, None]
    x_coord = ((2 * col_index + 1).astype(jnp.float32) / band_cols - 1.0)[None, :]
    numerator = jnp.zeros((tile_rows, tile_cols), jnp.float32)
    denominator = jnp.zeros((tile_rows, 1), jnp.float32)
    zero_value = jnp.zeros((), exposures.dtype)
    for member in range(exposures.shape[0]):
        first_row = row_start[member]
        row_total = row_count[member]
        inside = (row_index >= first_row) & (row_index < first_row + row_total)
        lead_row = row_base - 10 - first_row

        def placed_rows(window, portion, anchor, lead_row=lead_row):
            window_len = window.shape[0]
            portion_len = portion.shape[0]
            padding = jnp.zeros((window_len, portion.shape[1]), portion.dtype)
            extended = jnp.concatenate([padding, portion, padding], 0)
            sliced = lax.dynamic_slice_in_dim(extended, lead_row + window_len, window_len, 0)
            local_rows = lead_row + jnp.arange(window_len, dtype=jnp.int32)
            present = (local_rows >= 0) & (local_rows < portion_len)
            return jnp.where(present[:, None], sliced, window)

        empty_window = jnp.zeros((tile_rows + 20, tile_cols), exposures.dtype)
        window = placed_rows(
            empty_window,
            lax.all_gather(exposures[member], "narrow", axis=0, tiled=True),
            jnp.int32(0),
        )
        window_rows = row_base - 10 + jnp.arange(tile_rows + 20, dtype=jnp.int32)
        valid_rows = (window_rows >= first_row) & (window_rows < first_row + row_total)
        window = jnp.where(valid_rows[:, None], window, zero_value)
        window = padded(window, (("wide", 1),), 10)
        touches = (first_row < row_base + tile_rows) & (first_row + row_total > row_base)

        def matched_tile(window, member=member):
            response = respond(window, basis_kernels)
            matched = jnp.zeros((tile_rows, tile_cols), jnp.float32)
            for kernel in range(basis_kernels.shape[0]):
                coeffs = poly_coef[member, kernel]
                spatial = (
                    coeffs[0]
                    + coeffs[1] * x_coord
                    + coeffs[2] * y_coord
                    + coeffs[3] * x_coord * x_coord
                    + coeffs[4] * x_coord * y_coord
                    + coeffs[5] * y_coord * y_coord
                )
                matched = matched + spatial * response[kernel]
            return matched

        def empty_tile(window):
            return jnp.zeros((tile_rows, tile_cols), jnp.float32)

        matched = lax.cond(touches, matched_tile, empty_tile, window)
        weighting = exposure_weight[member] * inside.astype(jnp.float32)[:, None]
        numerator = numerator + weighting * matched
        denominator = denominator + weighting
    coadded = numerator / denominator
    taps_total = filter_taps.shape[0]
    framed = padded(coadded, (("wide", 1),), 10)
    inner = filter_taps[0] * framed[:, 0:tile_cols]
    for offset in range(1, taps_total):
        inner = inner + filter_taps[offset] * framed[:, offset : offset + tile_cols]
    across = padded(inner, (("narrow", 0),), 10)
    detection = filter_taps[0] * across[0:tile_rows]
    for offset in range(1, taps_total):
        detection = detection + filter_taps[offset] * across[offset : offset + tile_rows]
    return (coadded, detection)


def solution(mesh):
    placed = (P(None, "narrow", "wide"), P(), P(), P(), P(), P(), P())
    return jax.shard_map(
        on_device,
        mesh=mesh,
        in_specs=placed,
        out_specs=(P("narrow", "wide"), P("narrow", "wide")),
        check_vma=False,
    )
```

profile of v0, /device:TPU:384, one launch (start us, length us, event | category | flops | bytes accessed | tf_op | source)
XLA Modules:
  0.0 495.4 jit_solution(2599510035167982765)
XLA Ops:
  6.4 50.4 %all-gather.3 = bf16[1,512,384]{2,1,0:T(8,128)(2,1)S(1)} all-gather(bf16[1,32,384]{2,1,0:T(8,128)(2,1)S(1)} %get-tuple-element.333), channel_id=5, replica_groups=mesh['wide'=32,'narrow'=16] {'narrow'}, dimensions={1}, use_global_device_ids=true | all-gather | bytes 417792 | tf_op jit(solution)/shard_map/all_gather | solution.py:80
  59.7 2.4 collective-permute-start.6
  65.1 50.3 %all-gather = bf16[1,512,384]{2,1,0:T(8,128)(2,1)S(1)} all-gather(bf16[1,32,384]{2,1,0:T(8,128)(2,1)S(1)} %get-tuple-element.331), channel_id=2, replica_groups=mesh['wide'=32,'narrow'=16] {'narrow'}, dimensions={1}, use_global_device_ids=true | all-gather | bytes 417792 | tf_op jit(solution)/shard_map/all_gather | solution.py:80
  117.3 49.7 %all-gather.1 = bf16[1,512,384]{2,1,0:T(8,128)(2,1)S(1)} all-gather(bf16[1,32,384]{2,1,0:T(8,128)(2,1)S(1)} %get-tuple-element.332), channel_id=3, replica_groups=mesh['wide'=32,'narrow'=16] {'narrow'}, dimensions={1}, use_global_device_ids=true | all-gather | bytes 417792 | tf_op jit(solution)/shard_map/all_gather | solution.py:80
  168.3 49.0 %all-gather.2 = bf16[1,512,384]{2,1,0:T(8,128)(2,1)S(1)} all-gather(bf16[1,32,384]{2,1,0:T(8,128)(2,1)S(1)} %get-tuple-element.334), channel_id=4, replica_groups=mesh['wide'=32,'narrow'=16] {'narrow'}, dimensions={1}, use_global_device_ids=true | all-gather | bytes 417792 | tf_op jit(solution)/shard_map/all_gather | solution.py:80
  220.9 2.4 collective-permute-start.4
  223.4 5.3 %collective-permute-start.3 = (bf16[52,10]{1,0:T(8,128)(2,1)S(1)}, bf16[52,10]{1,0:T(8,128)(2,1)S(1)}, u32[]{:S(2)}, u32[]{:S(2)}) collective-permute-start(bf16[52,10]{1,0:T(8,128)(2,1)S(1)} %get-tuple-element.345), channel_id=1, source_target_pairs={{16,0},{32,16},{48,32},{64,48},{80,64},{96,80},{112,96},{128,112},... | collective-permute-start | bytes 3128 | tf_op jit(solution)/shard_map/ppermute | solution.py:16
  230.1 5.0 %add_add_fusion = (f32[32]{0:T(128)S(1)}, f32[32]{0:T(128)S(1)}, f32[32]{0:T(128)S(1)}, f32[32]{0:T(128)S(1)}, f32[32]{0:T(128)S(1)}) fusion(f32[]{:T(128)} %bitcast.314, s32[]{:T(128)S(6)} %add.1350, s32[]{:T(128)} %bitcast.312, s32[]{:T(128)S(6)} %mul.1366, f32[]{:T(128)} %bitcast.310, s32[]{:T(128)S(6)} %add.1334, s32[]{:T(128)} %bitcast.308, ...), kind=kLoop, calls=%fused_computation.570 | loop fusion | flops 640 | bytes 692 | tf_op jit(solution)/shard_map/add | solution.py:111
  237.8 1.9 collective-permute-start.2
  239.7 5.8 %collective-permute-start.1 = (bf16[52,10]{1,0:T(8,128)(2,1)S(1)}, bf16[52,10]{1,0:T(8,128)(2,1)S(1)}, u32[]{:S(2)}, u32[]{:S(2)}) collective-permute-start(bf16[52,10]{1,0:T(8,128)(2,1)S(1)} %get-tuple-element.340), channel_id=1, source_target_pairs={{16,0},{32,16},{48,32},{64,48},{80,64},{96,80},{112,96},{128,112},... | collective-permute-start | bytes 3128 | tf_op jit(solution)/shard_map/ppermute | solution.py:16
  245.6 1.9 collective-permute-start
  247.7 5.0 %collective-permute-done = bf16[52,10]{1,0:T(8,128)(2,1)S(1)} collective-permute-done((bf16[52,10]{1,0:T(8,128)(2,1)S(1)}, bf16[52,10]{1,0:T(8,128)(2,1)S(1)}, u32[]{:S(2)}, u32[]{:S(2)}) %collective-permute-start) | collective-permute-done | bytes 1072 | tf_op jit(solution)/shard_map/ppermute | solution.py:15
  252.8 48.0 %conditional.7 = (f32[32,384]{1,0:T(8,128)S(1)}) conditional(s32[]{:T(128)} %convert_element_type.81, () %tuple.38, (f32[4,5,6]{2,0,1:T(4,128)S(1)}, f32[1,384]{1,0:T(1,128)S(1)}, f32[32,1]{0,1:T(1,128)S(1)}, bf16[52,404]{1,0:T(8,128)(2,1)S(1)}, bf16[5,21,21]{2,1,0:T(8,128)(2,1)S(1)}) %tuple.324), branch_computations={%region_6.7_spmd, %region_7.8_spmd} | conditional | flops 470078048 | bytes 36717480 | solution.py:108
  254.2 3.9 copy.30
  258.1 8.9 %reshape.485 = bf16[21,148,640]{2,1,0:T(8,128)(2,1)} reshape(bf16[21,148,5,128]{3,2,1,0:T(8,128)(2,1)} %copy.30) | data formatting | bytes 7956480 | tf_op jit(solution)/shard_map/cond/branch_1_fun/reshape | solution.py:40
  267.0 8.8 %dot_general.38 = bf16[5,128,21,148]{1,0,3,2:T(8,128)(2,1)} reshape(bf16[640,21,148]{0,2,1:T(8,128)(2,1)} %bitcast.689) | data formatting | bytes 7956480 | tf_op jit(solution)/shard_map/cond/branch_1_fun/jarc,acn->jrn/dot_general | solution.py:41
  276.3 3.8 fusion.92
  281.8 6.2 %multiply_bitcast_fusion.19 = (f32[32]{0:T(128)S(1)}, f32[32]{0:T(128)S(1)}, f32[32]{0:T(128)S(1)}, f32[32]{0:T(128)S(1)}, f32[32]{0:T(128)S(1)}, /*index=5*/f32...) fusion(f32[32,1]{0,1:T(1,128)S(1)} %get-tuple-element.69, f32[]{:T(128)} %bitcast.233, ...), kind=kLoop, calls=%fused_computation.334 | loop fusion | flops 480 | bytes 1448 | tf_op jit(solution)/shard_map/cond/branch_1_fun/add | solution.py:95
  288.0 11.3 %add_reduce_fusion.19 = (f32[384]{0:T(512)S(1)}, f32[384]{0:T(512)S(1)}, f32[384]{0:T(512)S(1)}, f32[384]{0:T(512)S(1)}, f32[384]{0:T(512)S(1)}, /*index=5*/f32[...) fusion(f32[1,384]{1,0:T(1,128)S(1)} %get-tuple-element.68, ...), kind=kLoop, calls=%fused_computation.319 | loop fusion | flops 8448 | bytes 21576 | tf_op jit(solution)/shard_map/cond/branch_1_fun/add | solution.py:95
  300.8 48.2 %conditional.6 = (f32[32,384]{1,0:T(8,128)S(1)}) conditional(s32[]{:T(128)} %convert_element_type.80, () %tuple.36, (f32[4,5,6]{2,0,1:T(4,128)S(1)}, f32[1,384]{1,0:T(1,128)S(1)}, f32[32,1]{0,1:T(1,128)S(1)}, bf16[52,404]{1,0:T(8,128)(2,1)S(1)}, bf16[5,21,21]{2,1,0:T(8,128)(2,1)S(1)}) %tuple.325), branch_computations={%region_4.5_spmd, %region_5.6_spmd} | conditional | flops 470078048 | bytes 36717480 | solution.py:108
  302.4 3.9 copy.23
  306.3 8.9 %reshape.484 = bf16[21,148,640]{2,1,0:T(8,128)(2,1)} reshape(bf16[21,148,5,128]{3,2,1,0:T(8,128)(2,1)} %copy.23) | data formatting | bytes 7956480 | tf_op jit(solution)/shard_map/cond/branch_1_fun/reshape | solution.py:40
  315.2 8.8 %dot_general.34 = bf16[5,128,21,148]{1,0,3,2:T(8,128)(2,1)} reshape(bf16[640,21,148]{0,2,1:T(8,128)(2,1)} %bitcast.690) | data formatting | bytes 7956480 | tf_op jit(solution)/shard_map/cond/branch_1_fun/jarc,acn->jrn/dot_general | solution.py:41
  324.5 3.8 fusion.63
  330.0 6.3 %multiply_bitcast_fusion.14 = (f32[32]{0:T(128)S(1)}, f32[32]{0:T(128)S(1)}, f32[32]{0:T(128)S(1)}, f32[32]{0:T(128)S(1)}, f32[32]{0:T(128)S(1)}, /*index=5*/f32...) fusion(f32[32,1]{0,1:T(1,128)S(1)} %get-tuple-element.64, f32[]{:T(128)} %bitcast.156, ...), kind=kLoop, calls=%fused_computation.250 | loop fusion | flops 480 | bytes 1448 | tf_op jit(solution)/shard_map/cond/branch_1_fun/add | solution.py:95
  336.3 11.3 %add_reduce_fusion.14 = (f32[384]{0:T(512)S(1)}, f32[384]{0:T(512)S(1)}, f32[384]{0:T(512)S(1)}, f32[384]{0:T(512)S(1)}, f32[384]{0:T(512)S(1)}, /*index=5*/f32[...) fusion(f32[1,384]{1,0:T(1,128)S(1)} %get-tuple-element.63, ...), kind=kLoop, calls=%fused_computation.235 | loop fusion | flops 8448 | bytes 21576 | tf_op jit(solution)/shard_map/cond/branch_1_fun/add | solution.py:95
  349.0 48.2 %conditional.5 = (f32[32,384]{1,0:T(8,128)S(1)}) conditional(s32[]{:T(128)} %convert_element_type.79, () %tuple.34, (f32[4,5,6]{2,0,1:T(4,128)S(1)}, f32[1,384]{1,0:T(1,128)S(1)}, f32[32,1]{0,1:T(1,128)S(1)}, bf16[52,404]{1,0:T(8,128)(2,1)S(1)}, bf16[5,21,21]{2,1,0:T(8,128)(2,1)S(1)}) %tuple.326), branch_computations={%region_2.3_spmd, %region_3.4_spmd} | conditional | flops 470078048 | bytes 36717480 | solution.py:108
  350.6 3.9 copy.16
  354.5 8.9 %reshape.483 = bf16[21,148,640]{2,1,0:T(8,128)(2,1)} reshape(bf16[21,148,5,128]{3,2,1,0:T(8,128)(2,1)} %copy.16) | data formatting | bytes 7956480 | tf_op jit(solution)/shard_map/cond/branch_1_fun/reshape | solution.py:40
  363.4 8.8 %dot_general.26 = bf16[5,128,21,148]{1,0,3,2:T(8,128)(2,1)} reshape(bf16[640,21,148]{0,2,1:T(8,128)(2,1)} %bitcast.691) | data formatting | bytes 7956480 | tf_op jit(solution)/shard_map/cond/branch_1_fun/jarc,acn->jrn/dot_general | solution.py:41
  372.7 3.8 fusion.34
  378.2 6.2 %multiply_bitcast_fusion.9 = (f32[32]{0:T(128)S(1)}, f32[32]{0:T(128)S(1)}, f32[32]{0:T(128)S(1)}, f32[32]{0:T(128)S(1)}, f32[32]{0:T(128)S(1)}, /*index=5*/f32[...) fusion(f32[32,1]{0,1:T(1,128)S(1)} %get-tuple-element.59, f32[]{:T(128)} %bitcast.79, ...), kind=kLoop, calls=%fused_computation.166 | loop fusion | flops 480 | bytes 1448 | tf_op jit(solution)/shard_map/cond/branch_1_fun/add | solution.py:95
  384.5 11.2 %add_reduce_fusion.9 = (f32[384]{0:T(512)S(1)}, f32[384]{0:T(512)S(1)}, f32[384]{0:T(512)S(1)}, f32[384]{0:T(512)S(1)}, f32[384]{0:T(512)S(1)}, /*index=5*/f32[3...) fusion(f32[1,384]{1,0:T(1,128)S(1)} %get-tuple-element.58, ...), kind=kLoop, calls=%fused_computation.151 | loop fusion | flops 8448 | bytes 21576 | tf_op jit(solution)/shard_map/cond/branch_1_fun/add | solution.py:95
  397.2 48.2 %conditional.4 = (f32[32,384]{1,0:T(8,128)S(1)}) conditional(s32[]{:T(128)} %convert_element_type.76, () %tuple.32, (f32[4,5,6]{2,0,1:T(4,128)S(1)}, f32[1,384]{1,0:T(1,128)S(1)}, f32[32,1]{0,1:T(1,128)S(1)}, bf16[52,404]{1,0:T(8,128)(2,1)S(1)}, bf16[5,21,21]{2,1,0:T(8,128)(2,1)S(1)}) %tuple.327), branch_computations={%region_0.1_spmd, %region_1.2_spmd} | conditional | flops 470078048 | bytes 36717480 | solution.py:108
  398.8 3.9 copy.9
  402.7 8.9 %reshape.482 = bf16[21,148,640]{2,1,0:T(8,128)(2,1)} reshape(bf16[21,148,5,128]{3,2,1,0:T(8,128)(2,1)} %copy.9) | data formatting | bytes 7956480 | tf_op jit(solution)/shard_map/cond/branch_1_fun/reshape | solution.py:40
  411.6 8.8 %dot_general.18 = bf16[5,128,21,148]{1,0,3,2:T(8,128)(2,1)} reshape(bf16[640,21,148]{0,2,1:T(8,128)(2,1)} %bitcast.692) | data formatting | bytes 7956480 | tf_op jit(solution)/shard_map/cond/branch_1_fun/jarc,acn->jrn/dot_general | solution.py:41
  420.9 3.8 fusion.5
  426.4 6.2 %multiply_bitcast_fusion.4 = (f32[32]{0:T(128)S(1)}, f32[32]{0:T(128)S(1)}, f32[32]{0:T(128)S(1)}, f32[32]{0:T(128)S(1)}, f32[32]{0:T(128)S(1)}, /*index=5*/f32[...) fusion(f32[32,1]{0,1:T(1,128)S(1)} %get-tuple-element.48, f32[]{:T(128)} %bitcast.2, ...), kind=kLoop, calls=%fused_computation.82 | loop fusion | flops 480 | bytes 1448 | tf_op jit(solution)/shard_map/cond/branch_1_fun/add | solution.py:95
  432.7 11.2 %add_reduce_fusion.4 = (f32[384]{0:T(512)S(1)}, f32[384]{0:T(512)S(1)}, f32[384]{0:T(512)S(1)}, f32[384]{0:T(512)S(1)}, f32[384]{0:T(512)S(1)}, /*index=5*/f32[3...) fusion(f32[1,384]{1,0:T(1,128)S(1)} %get-tuple-element.47, ...), kind=kLoop, calls=%fused_computation.67 | loop fusion | flops 8448 | bytes 21576 | tf_op jit(solution)/shard_map/cond/branch_1_fun/add | solution.py:95
  445.6 1.9 collective-permute-start.9
  447.5 2.4 collective-permute-start.8
  450.6 4.1 collective-permute-done.8
  454.7 13.3 %fusion.119 = f32[32,384]{1,0:T(8,128)S(1)} fusion(f32[32,384]{1,0:T(8,128)S(1)} %add_divide_fusion, f32[32,10]{1,0:T(8,128)S(1)} %collective-permute-done.9, f32[32,10]{1,0:T(8,128)S(1)} %collective-permute-done.8, f32[]{:T(128)} %bitcast.344, f32[]{:T(128)} %bitcast.343, f32[]{:T(128)} %bitcast.342, f32[]{:T(128)} %bitcast.341, f32[]{:T(128)} %bitcast.340, ...), kind=kLoop, calls=%fused_computation.427 | loop fusion | flops 749568 | bytes 100948 | tf_op jit(solution)/shard_map/add | solution.py:117
  468.0 1.9 collective-permute-start.11
  469.9 3.9 collective-permute-start.10
  473.9 7.8 %collective-permute-done.10 = f32[10,384]{1,0:T(8,128)S(1)} collective-permute-done((f32[10,384]{1,0:T(8,128)S(1)}, f32[10,384]{1,0:T(8,128)S(1)}, u32[]{:S(2)}, u32[]{:S(2)}) %collective-permute-start.10) | collective-permute-done | bytes 15392 | tf_op jit(solution)/shard_map/ppermute | solution.py:15
  481.7 13.7 %fusion.175 = f32[32,384]{1,0:T(8,128)} fusion(f32[32,384]{1,0:T(8,128)S(1)} %fusion.119, f32[10,384]{1,0:T(8,128)S(1)} %collective-permute-done.11, f32[10,384]{1,0:T(8,128)S(1)} %collective-permute-done.10, f32[]{:T(128)} %bitcast.344, f32[]{:T(128)} %bitcast.343, f32[]{:T(128)} %bitcast.342, f32[]{:T(128)} %bitcast.341, f32[]{:T(128)} %bitcast.340, ...), kind=kLoop, calls=%fused_computation.483 | loop fusion | flops 749568 | bytes 129108 | tf_op jit(solution)/shard_map/add | solution.py:121
  (183 shorter events, 32.7 us)
Async XLA Ops:
  0.6 228.1 %copy-start.4 = (f32[4]{0:T(128)S(1)}, f32[4]{0:T(128)}, u32[]{:S(2)}) copy-start(f32[4]{0:T(128)} %param.18) | copy-start | bytes 52
  0.6 228.8 %copy-start.3 = (f32[21]{0:T(128)S(1)}, f32[21]{0:T(128)}, u32[]{:S(2)}) copy-start(f32[21]{0:T(128)} %param.21) | copy-start | bytes 256
  0.7 252.2 %copy-start.1 = (f32[4,5,6]{2,0,1:T(4,128)S(1)}, f32[4,5,6]{2,0,1:T(4,128)}, u32[]{:S(2)}) copy-start(f32[4,5,6]{2,0,1:T(4,128)} %param.17) | copy-start | bytes 1444
  0.7 252.2 %copy-start = (bf16[5,21,21]{2,1,0:T(8,128)(2,1)S(1)}, bf16[5,21,21]{2,1,0:T(8,128)(2,1)}, u32[]{:S(2)}) copy-start(bf16[5,21,21]{2,1,0:T(8,128)(2,1)} %param.16) | copy-start | bytes 13234
  57.7 180.0 %collective-permute-start.7 = (bf16[52,10]{1,0:T(8,128)(2,1)S(1)}, bf16[52,10]{1,0:T(8,128)(2,1)S(1)}, u32[]{:S(2)}, u32[]{:S(2)}) collective-permute-start(bf16[52,10]{1,0:T(8,128)(2,1)S(1)} %get-tuple-element.349), channel_id=1, source_target_pairs={{16,0},{32,16},{48,32},{64,48},{80,64},{96,80},{112,96},{128,112},... | collective-permute-start | bytes 3128 | tf_op jit(solution)/shard_map/ppermute | solution.py:16
  59.7 180.0 %collective-permute-start.6 = (bf16[52,10]{1,0:T(8,128)(2,1)S(1)}, bf16[52,10]{1,0:T(8,128)(2,1)S(1)}, u32[]{:S(2)}, u32[]{:S(2)}) collective-permute-start(bf16[52,10]{1,0:T(8,128)(2,1)S(1)} %get-tuple-element.348), channel_id=1, source_target_pairs={{0,16},{16,32},{32,48},{48,64},{64,80},{80,96},{96,112},{112,128},... | collective-permute-start | bytes 3128 | tf_op jit(solution)/shard_map/ppermute | solution.py:15
  219.0 26.6 %collective-permute-start.5 = (bf16[52,10]{1,0:T(8,128)(2,1)S(1)}, bf16[52,10]{1,0:T(8,128)(2,1)S(1)}, u32[]{:S(2)}, u32[]{:S(2)}) collective-permute-start(bf16[52,10]{1,0:T(8,128)(2,1)S(1)} %get-tuple-element.347), channel_id=1, source_target_pairs={{16,0},{32,16},{48,32},{64,48},{80,64},{96,80},{112,96},{128,112},... | collective-permute-start | bytes 3128 | tf_op jit(solution)/shard_map/ppermute | solution.py:16
  220.9 26.6 %collective-permute-start.4 = (bf16[52,10]{1,0:T(8,128)(2,1)S(1)}, bf16[52,10]{1,0:T(8,128)(2,1)S(1)}, u32[]{:S(2)}, u32[]{:S(2)}) collective-permute-start(bf16[52,10]{1,0:T(8,128)(2,1)S(1)} %get-tuple-element.346), channel_id=1, source_target_pairs={{0,16},{16,32},{32,48},{48,64},{64,80},{80,96},{96,112},{112,128},... | collective-permute-start | bytes 3128 | tf_op jit(solution)/shard_map/ppermute | solution.py:15
  223.4 24.2 %collective-permute-start.3 = (bf16[52,10]{1,0:T(8,128)(2,1)S(1)}, bf16[52,10]{1,0:T(8,128)(2,1)S(1)}, u32[]{:S(2)}, u32[]{:S(2)}) collective-permute-start(bf16[52,10]{1,0:T(8,128)(2,1)S(1)} %get-tuple-element.345), channel_id=1, source_target_pairs={{16,0},{32,16},{48,32},{64,48},{80,64},{96,80},{112,96},{128,112},... | collective-permute-start | bytes 3128 | tf_op jit(solution)/shard_map/ppermute | solution.py:16
  237.8 9.9 %collective-permute-start.2 = (bf16[52,10]{1,0:T(8,128)(2,1)S(1)}, bf16[52,10]{1,0:T(8,128)(2,1)S(1)}, u32[]{:S(2)}, u32[]{:S(2)}) collective-permute-start(bf16[52,10]{1,0:T(8,128)(2,1)S(1)} %get-tuple-element.344), channel_id=1, source_target_pairs={{0,16},{16,32},{32,48},{48,64},{64,80},{80,96},{96,112},{112,128},... | collective-permute-start | bytes 3128 | tf_op jit(solution)/shard_map/ppermute | solution.py:15
  239.7 8.0 %collective-permute-start.1 = (bf16[52,10]{1,0:T(8,128)(2,1)S(1)}, bf16[52,10]{1,0:T(8,128)(2,1)S(1)}, u32[]{:S(2)}, u32[]{:S(2)}) collective-permute-start(bf16[52,10]{1,0:T(8,128)(2,1)S(1)} %get-tuple-element.340), channel_id=1, source_target_pairs={{16,0},{32,16},{48,32},{64,48},{80,64},{96,80},{112,96},{128,112},... | collective-permute-start | bytes 3128 | tf_op jit(solution)/shard_map/ppermute | solution.py:16
  245.6 7.1 %collective-permute-start = (bf16[52,10]{1,0:T(8,128)(2,1)S(1)}, bf16[52,10]{1,0:T(8,128)(2,1)S(1)}, u32[]{:S(2)}, u32[]{:S(2)}) collective-permute-start(bf16[52,10]{1,0:T(8,128)(2,1)S(1)} %get-tuple-element.339), channel_id=1, source_target_pairs={{0,16},{16,32},{32,48},{48,64},{64,80},{80,96},{96,112},{112,128},... | collective-permute-start | bytes 3128 | tf_op jit(solution)/shard_map/ppermute | solution.py:15
  445.5 49.9 %copy-start.2 = (f32[32,384]{1,0:T(8,128)}, f32[32,384]{1,0:T(8,128)S(1)}, u32[]{:S(2)}) copy-start(f32[32,384]{1,0:T(8,128)S(1)} %add_divide_fusion) | copy-start | bytes 147460
  445.6 5.0 %collective-permute-start.9 = (f32[32,10]{1,0:T(8,128)S(1)}, f32[32,10]{1,0:T(8,128)S(1)}, u32[]{:S(2)}, u32[]{:S(2)}) collective-permute-start(f32[32,10]{1,0:T(8,128)S(1)} %get-tuple-element.338), channel_id=1, source_target_pairs={{16,0},{32,16},{48,32},{64,48},{80,64},{96,80},{112,96},{128,112},... | collective-permute-start | bytes 3848 | tf_op jit(solution)/shard_map/ppermute | solution.py:16
  447.5 7.2 %collective-permute-start.8 = (f32[32,10]{1,0:T(8,128)S(1)}, f32[32,10]{1,0:T(8,128)S(1)}, u32[]{:S(2)}, u32[]{:S(2)}) collective-permute-start(f32[32,10]{1,0:T(8,128)S(1)} %get-tuple-element.337), channel_id=1, source_target_pairs={{0,16},{16,32},{32,48},{48,64},{64,80},{80,96},{96,112},{112,128},... | collective-permute-start | bytes 3848 | tf_op jit(solution)/shard_map/ppermute | solution.py:15
  468.0 5.9 %collective-permute-start.11 = (f32[10,384]{1,0:T(8,128)S(1)}, f32[10,384]{1,0:T(8,128)S(1)}, u32[]{:S(2)}, u32[]{:S(2)}) collective-permute-start(f32[10,384]{1,0:T(8,128)S(1)} %get-tuple-element.336), channel_id=1, source_target_pairs={{1,0},{2,1},{3,2},{4,3},{5,4},{6,5},{7,6},{8,7},{9,8},{10,9},{11,1... | collective-permute-start | bytes 46088 | tf_op jit(solution)/shard_map/ppermute | solution.py:16
  469.9 11.7 %collective-permute-start.10 = (f32[10,384]{1,0:T(8,128)S(1)}, f32[10,384]{1,0:T(8,128)S(1)}, u32[]{:S(2)}, u32[]{:S(2)}) collective-permute-start(f32[10,384]{1,0:T(8,128)S(1)} %get-tuple-element.335), channel_id=1, source_target_pairs={{0,1},{1,2},{2,3},{3,4},{4,5},{5,6},{6,7},{7,8},{8,9},{9,10},{10,1... | collective-permute-start | bytes 46088 | tf_op jit(solution)/shard_map/ppermute | solution.py:15
where the time goes:
time: 499 us; the launch traced here: 495 us
  blocking collectives  199 us (40%)
  other arithmetic  111 us (22%)
  local copies, waits for them, and re-layouts  100 us (20%)
  starting transfers between devices  33.6 us (7%)
  matrix products  20.7 us (4%)
  waiting for transfers between devices  16.9 us (3%)
  between operations  11.2 us (2%)
    all_gather x4, blocking collectives, on_device(): lax.all_gather(exposures[member], 'narrow', axis=0, tiled=True)  199 us
    add x8, other arithmetic, matched_tile(): coeffs[0] + coeffs[1] * x_coord + coeffs[2] * y_coord  69.9 us
    reshape x4, local copies, waits for them, and re-layouts, respond(): table = table.astype(jnp.bfloat16).reshape(side, span, kernel_total * block)  35.6 us
    dot_general x4, local copies, waits for them, and re-layouts, respond(): jnp.einsum('jarc,acn->jrn', patches, table, preferred_element_type=jnp.fl...  35.1 us
    ppermute x6, starting transfers between devices, padded(): after = lax.ppermute(initial, axis, down)  18.7 us
    ppermute x6, waiting for transfers between devices, padded(): before = lax.ppermute(last, axis, up)  16.9 us
    convert_element_type x4, local copies, waits for them, and re-layouts, respond(): table = table.astype(jnp.bfloat16).reshape(side, span, kernel_total * block)  15.6 us
    dot_general x4, matrix products, respond(): jnp.einsum('jarc,acn->jrn', patches, table, preferred_element_type=jnp.fl...  15.4 us
  transfers between devices with their start and end apart: 12, of which 3 were waited for; matrix products, arithmetic and copies ran while one was open for 2% of the time, Pallas kernels for 0%

commit v1 on v0

--- a/solution.py
+++ b/solution.py
@@ -77,7 +77,12 @@
         empty_window = jnp.zeros((tile_rows + 20, tile_cols), exposures.dtype)
         window = placed_rows(
             empty_window,
-            lax.all_gather(exposures[member], "narrow", axis=0, tiled=True),
+            jnp.concatenate(
+                lax.all_to_all(
+                    jnp.stack([exposures[member]] * lax.axis_size("narrow")), "narrow", 0, 0
+                ),
+                axis=0,
+            ),
             jnp.int32(0),
         )
         window_rows = row_base - 10 + jnp.arange(tile_rows + 20, dtype=jnp.int32)

time: 499 us -> 368 us (0.74)
  the two profiles are of different devices: /device:TPU:384 before, /device:TPU:448 now
where the time goes in v1:
time: 368 us; the launch traced here: 364 us
  other arithmetic  111 us (30%)
  local copies, waits for them, and re-layouts  104 us (28%)
  starting transfers between devices  68.8 us (19%)
  blocking collectives  24.1 us (7%)
  waiting for transfers between devices  22.5 us (6%)
  matrix products  20.7 us (6%)
  between operations  11.2 us (3%)
    add x8, other arithmetic, matched_tile(): coeffs[0] + coeffs[1] * x_coord + coeffs[2] * y_coord  69.8 us
    reshape x4, local copies, waits for them, and re-layouts, respond(): table = table.astype(jnp.bfloat16).reshape(side, span, kernel_total * block)  35.6 us
    dot_general x4, local copies, waits for them, and re-layouts, respond(): jnp.einsum('jarc,acn->jrn', patches, table, preferred_element_type=jnp.fl...  35.1 us
    all_to_all x3, starting transfers between devices, on_device(): lax.all_to_all(jnp.stack([exposures[member]] * lax.axis_size('narrow')),...  30.6 us
    ppermute x6, starting transfers between devices, padded(): after = lax.ppermute(initial, axis, down)  24.2 us
    all_to_all x1, blocking collectives, on_device(): lax.all_to_all(jnp.stack([exposures[member]] * lax.axis_size('narrow')),...  24.1 us
    ppermute x6, waiting for transfers between devices, padded(): before = lax.ppermute(last, axis, up)  16.9 us
    convert_element_type x4, local copies, waits for them, and re-layouts, respond(): table = table.astype(jnp.bfloat16).reshape(side, span, kernel_total * block)  15.6 us
  transfers between devices with their start and end apart: 15, of which 5 were waited for; matrix products, arithmetic and copies ran while one was open for 4% of the time, Pallas kernels for 0%

profile of v1, /device:TPU:448, one launch (start us, length us, event | category | flops | bytes accessed | tf_op | source)
XLA Modules:
  0.0 363.7 jit_solution(12662371495738432425)
XLA Ops:
  1.5 24.1 %all_to_all.20 = bf16[16,32,384]{2,1,0:T(8,128)(2,1)S(1)} all-to-all(bf16[16,32,384]{2,1,0:T(8,128)(2,1)S(1)} %stack.327), channel_id=1, replica_groups=mesh['wide'=32,'narrow'=16] {'narrow'}, dimensions={0} | all-to-all | bytes 786432 | tf_op jit(solution)/shard_map/all_to_all | solution.py:81
  26.4 9.5 %all-to-all-start = ((bf16[16,32,384]{2,1,0:T(8,128)(2,1)}), bf16[16,32,384]{2,1,0:T(8,128)(2,1)S(1)}, u32[]{:S(2)}, u32[]{:S(2)}) async-start(bf16[16,32,384]{2,1,0:T(8,128)(2,1)} %stack.324), calls=%async_computation | async-start | bytes 786432 | tf_op jit(solution)/shard_map/all_to_all | solution.py:81
  42.5 5.1 %all-to-all-done = bf16[16,32,384]{2,1,0:T(8,128)(2,1)S(1)} async-done(((bf16[16,32,384]{2,1,0:T(8,128)(2,1)}), bf16[16,32,384]{2,1,0:T(8,128)(2,1)S(1)}, u32[]{:S(2)}, u32[]{:S(2)}) %all-to-all-start) | async-done | bytes 393248 | tf_op jit(solution)/shard_map/all_to_all | solution.py:81
  48.3 9.5 %all-to-all-start.1 = ((bf16[16,32,384]{2,1,0:T(8,128)(2,1)}), bf16[16,32,384]{2,1,0:T(8,128)(2,1)S(1)}, u32[]{:S(2)}, u32[]{:S(2)}) async-start(bf16[16,32,384]{2,1,0:T(8,128)(2,1)} %stack.325), calls=%async_computation.1 | async-start | bytes 786432 | tf_op jit(solution)/shard_map/all_to_all | solution.py:81
  69.8 11.5 %all-to-all-start.2 = ((bf16[16,32,384]{2,1,0:T(8,128)(2,1)}), bf16[16,32,384]{2,1,0:T(8,128)(2,1)S(1)}, u32[]{:S(2)}, u32[]{:S(2)}) async-start(bf16[16,32,384]{2,1,0:T(8,128)(2,1)} %stack.326), calls=%async_computation.2 | async-start | bytes 786432 | tf_op jit(solution)/shard_map/all_to_all | solution.py:81
  81.3 5.0 %add_add_fusion = (f32[32]{0:T(128)S(1)}, f32[32]{0:T(128)S(1)}, f32[32]{0:T(128)S(1)}, f32[32]{0:T(128)S(1)}, f32[32]{0:T(128)S(1)}) fusion(f32[]{:T(128)} %bitcast.315, s32[]{:T(128)S(6)} %add.1350, s32[]{:T(128)} %bitcast.313, s32[]{:T(128)S(6)} %mul.1366, f32[]{:T(128)} %bitcast.310, s32[]{:T(128)S(6)} %add.1334, s32[]{:T(128)} %bitcast.308, ...), kind=kLoop, calls=%fused_computation.574 | loop fusion | flops 640 | bytes 692 | tf_op jit(solution)/shard_map/add | solution.py:116
  87.2 3.1 collective-permute-start.7
  90.4 1.9 collective-permute-start.6
  92.7 5.7 %collective-permute-start.5 = (bf16[52,10]{1,0:T(8,128)(2,1)S(1)}, bf16[52,10]{1,0:T(8,128)(2,1)S(1)}, u32[]{:S(2)}, u32[]{:S(2)}) collective-permute-start(bf16[52,10]{1,0:T(8,128)(2,1)S(1)} %get-tuple-element.347), channel_id=1, source_target_pairs={{16,0},{32,16},{48,32},{64,48},{80,64},{96,80},{112,96},{128,112},... | collective-permute-start | bytes 3128 | tf_op jit(solution)/shard_map/ppermute | solution.py:16
  98.5 1.9 collective-permute-start.4
  100.5 5.7 %collective-permute-start.3 = (bf16[52,10]{1,0:T(8,128)(2,1)S(1)}, bf16[52,10]{1,0:T(8,128)(2,1)S(1)}, u32[]{:S(2)}, u32[]{:S(2)}) collective-permute-start(bf16[52,10]{1,0:T(8,128)(2,1)S(1)} %get-tuple-element.345), channel_id=1, source_target_pairs={{16,0},{32,16},{48,32},{64,48},{80,64},{96,80},{112,96},{128,112},... | collective-permute-start | bytes 3128 | tf_op jit(solution)/shard_map/ppermute | solution.py:16
  108.2 5.8 %collective-permute-start.1 = (bf16[52,10]{1,0:T(8,128)(2,1)S(1)}, bf16[52,10]{1,0:T(8,128)(2,1)S(1)}, u32[]{:S(2)}, u32[]{:S(2)}) collective-permute-start(bf16[52,10]{1,0:T(8,128)(2,1)S(1)} %get-tuple-element.340), channel_id=1, source_target_pairs={{16,0},{32,16},{48,32},{64,48},{80,64},{96,80},{112,96},{128,112},... | collective-permute-start | bytes 3128 | tf_op jit(solution)/shard_map/ppermute | solution.py:16
  114.1 1.9 collective-permute-start
  116.3 5.0 %collective-permute-done = bf16[52,10]{1,0:T(8,128)(2,1)S(1)} collective-permute-done((bf16[52,10]{1,0:T(8,128)(2,1)S(1)}, bf16[52,10]{1,0:T(8,128)(2,1)S(1)}, u32[]{:S(2)}, u32[]{:S(2)}) %collective-permute-start) | collective-permute-done | bytes 1072 | tf_op jit(solution)/shard_map/ppermute | solution.py:15
  121.4 47.9 %conditional.7 = (f32[32,384]{1,0:T(8,128)S(1)}) conditional(s32[]{:T(128)} %convert_element_type.81, () %tuple.38, (f32[4,5,6]{2,0,1:T(4,128)S(1)}, f32[1,384]{1,0:T(1,128)S(1)}, f32[32,1]{0,1:T(1,128)S(1)}, bf16[52,404]{1,0:T(8,128)(2,1)S(1)}, bf16[5,21,21]{2,1,0:T(8,128)(2,1)S(1)}) %tuple.324), branch_computations={%region_6.7_spmd, %region_7.8_spmd} | conditional | flops 470078048 | bytes 36717480 | solution.py:113
  122.7 3.9 %copy.30 = bf16[21,148,5,128]{3,2,1,0:T(8,128)(2,1)} copy(bf16[21,148,5,128]{3,0,2,1:T(8,128)(2,1)S(1)} %convert_bitcast_fusion.3) | data formatting | bytes 7956480 | tf_op jit(solution)/shard_map/cond/branch_1_fun/convert_element_type | solution.py:40
  126.6 8.9 %reshape.497 = bf16[21,148,640]{2,1,0:T(8,128)(2,1)} reshape(bf16[21,148,5,128]{3,2,1,0:T(8,128)(2,1)} %copy.30) | data formatting | bytes 7956480 | tf_op jit(solution)/shard_map/cond/branch_1_fun/reshape | solution.py:40
  135.5 8.8 %dot_general.38 = bf16[5,128,21,148]{1,0,3,2:T(8,128)(2,1)} reshape(bf16[640,21,148]{0,2,1:T(8,128)(2,1)} %bitcast.697) | data formatting | bytes 7956480 | tf_op jit(solution)/shard_map/cond/branch_1_fun/jarc,acn->jrn/dot_general | solution.py:41
  144.8 3.8 %fusion.92 = f32[5,32,3,128]{3,1,0,2:T(8,128)S(1)} fusion(bf16[5,128,21,148]{1,0,3,2:T(8,128)(2,1)} %dot_general.38, bf16[1,21,32,148]{3,2,1,0:T(8,128)(2,1)S(1)} %get-tuple-element.284, bf16[1,21,32,148]{3,2,1,0:T(8,128)(2,1)S(1)} %get-tuple-element.285, bf16[1,21,32,148]{3,2,1,0:T(8,128)(2,1)S(1)} %get-tuple-element.283), kind=kOutput, calls=%fused_computation.258 | convolution fusion | flops 383701248 | bytes 4820736 | tf_op jit(solution)/shard_map/cond/branch_1_fun/jarc,acn->jrn/dot_general | solution.py:41
  150.4 6.2 %multiply_bitcast_fusion.19 = (f32[32]{0:T(128)S(1)}, f32[32]{0:T(128)S(1)}, f32[32]{0:T(128)S(1)}, f32[32]{0:T(128)S(1)}, f32[32]{0:T(128)S(1)}, /*index=5*/f32...) fusion(f32[32,1]{0,1:T(1,128)S(1)} %get-tuple-element.69, f32[]{:T(128)} %bitcast.233, ...), kind=kLoop, calls=%fused_computation.334 | loop fusion | flops 480 | bytes 1448 | tf_op jit(solution)/shard_map/cond/branch_1_fun/add | solution.py:100
  156.6 11.2 %add_reduce_fusion.19 = (f32[384]{0:T(512)S(1)}, f32[384]{0:T(512)S(1)}, f32[384]{0:T(512)S(1)}, f32[384]{0:T(512)S(1)}, f32[384]{0:T(512)S(1)}, /*index=5*/f32[...) fusion(f32[1,384]{1,0:T(1,128)S(1)} %get-tuple-element.68, ...), kind=kLoop, calls=%fused_computation.319 | loop fusion | flops 8448 | bytes 21576 | tf_op jit(solution)/shard_map/cond/branch_1_fun/add | solution.py:100
  169.3 48.1 %conditional.6 = (f32[32,384]{1,0:T(8,128)S(1)}) conditional(s32[]{:T(128)} %convert_element_type.80, () %tuple.36, (f32[4,5,6]{2,0,1:T(4,128)S(1)}, f32[1,384]{1,0:T(1,128)S(1)}, f32[32,1]{0,1:T(1,128)S(1)}, bf16[52,404]{1,0:T(8,128)(2,1)S(1)}, bf16[5,21,21]{2,1,0:T(8,128)(2,1)S(1)}) %tuple.325), branch_computations={%region_4.5_spmd, %region_5.6_spmd} | conditional | flops 470078048 | bytes 36717480 | solution.py:113
  170.9 3.9 %copy.23 = bf16[21,148,5,128]{3,2,1,0:T(8,128)(2,1)} copy(bf16[21,148,5,128]{3,0,2,1:T(8,128)(2,1)S(1)} %convert_bitcast_fusion.2) | data formatting | bytes 7956480 | tf_op jit(solution)/shard_map/cond/branch_1_fun/convert_element_type | solution.py:40
  174.8 8.9 %reshape.496 = bf16[21,148,640]{2,1,0:T(8,128)(2,1)} reshape(bf16[21,148,5,128]{3,2,1,0:T(8,128)(2,1)} %copy.23) | data formatting | bytes 7956480 | tf_op jit(solution)/shard_map/cond/branch_1_fun/reshape | solution.py:40
  183.7 8.8 %dot_general.34 = bf16[5,128,21,148]{1,0,3,2:T(8,128)(2,1)} reshape(bf16[640,21,148]{0,2,1:T(8,128)(2,1)} %bitcast.698) | data formatting | bytes 7956480 | tf_op jit(solution)/shard_map/cond/branch_1_fun/jarc,acn->jrn/dot_general | solution.py:41
  193.0 3.8 %fusion.63 = f32[5,32,3,128]{3,1,0,2:T(8,128)S(1)} fusion(bf16[5,128,21,148]{1,0,3,2:T(8,128)(2,1)} %dot_general.34, bf16[1,21,32,148]{3,2,1,0:T(8,128)(2,1)S(1)} %get-tuple-element.236, bf16[1,21,32,148]{3,2,1,0:T(8,128)(2,1)S(1)} %get-tuple-element.237, bf16[1,21,32,148]{3,2,1,0:T(8,128)(2,1)S(1)} %get-tuple-element.235), kind=kOutput, calls=%fused_computation.174 | convolution fusion | flops 383701248 | bytes 4820736 | tf_op jit(solution)/shard_map/cond/branch_1_fun/jarc,acn->jrn/dot_general | solution.py:41
  198.5 6.2 %multiply_bitcast_fusion.14 = (f32[32]{0:T(128)S(1)}, f32[32]{0:T(128)S(1)}, f32[32]{0:T(128)S(1)}, f32[32]{0:T(128)S(1)}, f32[32]{0:T(128)S(1)}, /*index=5*/f32...) fusion(f32[32,1]{0,1:T(1,128)S(1)} %get-tuple-element.64, f32[]{:T(128)} %bitcast.156, ...), kind=kLoop, calls=%fused_computation.250 | loop fusion | flops 480 | bytes 1448 | tf_op jit(solution)/shard_map/cond/branch_1_fun/add | solution.py:100
  204.7 11.2 %add_reduce_fusion.14 = (f32[384]{0:T(512)S(1)}, f32[384]{0:T(512)S(1)}, f32[384]{0:T(512)S(1)}, f32[384]{0:T(512)S(1)}, f32[384]{0:T(512)S(1)}, /*index=5*/f32[...) fusion(f32[1,384]{1,0:T(1,128)S(1)} %get-tuple-element.63, ...), kind=kLoop, calls=%fused_computation.235 | loop fusion | flops 8448 | bytes 21576 | tf_op jit(solution)/shard_map/cond/branch_1_fun/add | solution.py:100
  217.4 48.2 %conditional.5 = (f32[32,384]{1,0:T(8,128)S(1)}) conditional(s32[]{:T(128)} %convert_element_type.79, () %tuple.34, (f32[4,5,6]{2,0,1:T(4,128)S(1)}, f32[1,384]{1,0:T(1,128)S(1)}, f32[32,1]{0,1:T(1,128)S(1)}, bf16[52,404]{1,0:T(8,128)(2,1)S(1)}, bf16[5,21,21]{2,1,0:T(8,128)(2,1)S(1)}) %tuple.326), branch_computations={%region_2.3_spmd, %region_3.4_spmd} | conditional | flops 470078048 | bytes 36717480 | solution.py:113
  219.0 3.9 %copy.16 = bf16[21,148,5,128]{3,2,1,0:T(8,128)(2,1)} copy(bf16[21,148,5,128]{3,0,2,1:T(8,128)(2,1)S(1)} %convert_bitcast_fusion.1) | data formatting | bytes 7956480 | tf_op jit(solution)/shard_map/cond/branch_1_fun/convert_element_type | solution.py:40
  222.9 8.9 %reshape.495 = bf16[21,148,640]{2,1,0:T(8,128)(2,1)} reshape(bf16[21,148,5,128]{3,2,1,0:T(8,128)(2,1)} %copy.16) | data formatting | bytes 7956480 | tf_op jit(solution)/shard_map/cond/branch_1_fun/reshape | solution.py:40
  231.8 8.8 %dot_general.26 = bf16[5,128,21,148]{1,0,3,2:T(8,128)(2,1)} reshape(bf16[640,21,148]{0,2,1:T(8,128)(2,1)} %bitcast.699) | data formatting | bytes 7956480 | tf_op jit(solution)/shard_map/cond/branch_1_fun/jarc,acn->jrn/dot_general | solution.py:41
  241.1 3.8 %fusion.34 = f32[5,32,3,128]{3,1,0,2:T(8,128)S(1)} fusion(bf16[5,128,21,148]{1,0,3,2:T(8,128)(2,1)} %dot_general.26, bf16[1,21,32,148]{3,2,1,0:T(8,128)(2,1)S(1)} %get-tuple-element.188, bf16[1,21,32,148]{3,2,1,0:T(8,128)(2,1)S(1)} %get-tuple-element.189, bf16[1,21,32,148]{3,2,1,0:T(8,128)(2,1)S(1)} %get-tuple-element.187), kind=kOutput, calls=%fused_computation.90 | convolution fusion | flops 383701248 | bytes 4820736 | tf_op jit(solution)/shard_map/cond/branch_1_fun/jarc,acn->jrn/dot_general | solution.py:41
  246.6 6.2 %multiply_bitcast_fusion.9 = (f32[32]{0:T(128)S(1)}, f32[32]{0:T(128)S(1)}, f32[32]{0:T(128)S(1)}, f32[32]{0:T(128)S(1)}, f32[32]{0:T(128)S(1)}, /*index=5*/f32[...) fusion(f32[32,1]{0,1:T(1,128)S(1)} %get-tuple-element.59, f32[]{:T(128)} %bitcast.79, ...), kind=kLoop, calls=%fused_computation.166 | loop fusion | flops 480 | bytes 1448 | tf_op jit(solution)/shard_map/cond/branch_1_fun/add | solution.py:100
  252.9 11.2 %add_reduce_fusion.9 = (f32[384]{0:T(512)S(1)}, f32[384]{0:T(512)S(1)}, f32[384]{0:T(512)S(1)}, f32[384]{0:T(512)S(1)}, f32[384]{0:T(512)S(1)}, /*index=5*/f32[3...) fusion(f32[1,384]{1,0:T(1,128)S(1)} %get-tuple-element.58, ...), kind=kLoop, calls=%fused_computation.151 | loop fusion | flops 8448 | bytes 21576 | tf_op jit(solution)/shard_map/cond/branch_1_fun/add | solution.py:100
  265.6 48.2 %conditional.4 = (f32[32,384]{1,0:T(8,128)S(1)}) conditional(s32[]{:T(128)} %convert_element_type.76, () %tuple.32, (f32[4,5,6]{2,0,1:T(4,128)S(1)}, f32[1,384]{1,0:T(1,128)S(1)}, f32[32,1]{0,1:T(1,128)S(1)}, bf16[52,404]{1,0:T(8,128)(2,1)S(1)}, bf16[5,21,21]{2,1,0:T(8,128)(2,1)S(1)}) %tuple.327), branch_computations={%region_0.1_spmd, %region_1.2_spmd} | conditional | flops 470078048 | bytes 36717480 | solution.py:113
  267.2 3.9 %copy.9 = bf16[21,148,5,128]{3,2,1,0:T(8,128)(2,1)} copy(bf16[21,148,5,128]{3,0,2,1:T(8,128)(2,1)S(1)} %convert_bitcast_fusion) | data formatting | bytes 7956480 | tf_op jit(solution)/shard_map/cond/branch_1_fun/convert_element_type | solution.py:40
  271.1 8.9 %reshape.494 = bf16[21,148,640]{2,1,0:T(8,128)(2,1)} reshape(bf16[21,148,5,128]{3,2,1,0:T(8,128)(2,1)} %copy.9) | data formatting | bytes 7956480 | tf_op jit(solution)/shard_map/cond/branch_1_fun/reshape | solution.py:40
  280.0 8.8 %dot_general.18 = bf16[5,128,21,148]{1,0,3,2:T(8,128)(2,1)} reshape(bf16[640,21,148]{0,2,1:T(8,128)(2,1)} %bitcast.700) | data formatting | bytes 7956480 | tf_op jit(solution)/shard_map/cond/branch_1_fun/jarc,acn->jrn/dot_general | solution.py:41
  289.3 3.8 %fusion.5 = f32[5,32,3,128]{3,1,0,2:T(8,128)S(1)} fusion(bf16[5,128,21,148]{1,0,3,2:T(8,128)(2,1)} %dot_general.18, bf16[1,21,32,148]{3,2,1,0:T(8,128)(2,1)S(1)} %get-tuple-element.140, bf16[1,21,32,148]{3,2,1,0:T(8,128)(2,1)S(1)} %get-tuple-element.141, bf16[1,21,32,148]{3,2,1,0:T(8,128)(2,1)S(1)} %get-tuple-element.139), kind=kOutput, calls=%fused_computation.6 | convolution fusion | flops 383701248 | bytes 4820736 | tf_op jit(solution)/shard_map/cond/branch_1_fun/jarc,acn->jrn/dot_general | solution.py:41
  294.9 6.2 %multiply_bitcast_fusion.4 = (f32[32]{0:T(128)S(1)}, f32[32]{0:T(128)S(1)}, f32[32]{0:T(128)S(1)}, f32[32]{0:T(128)S(1)}, f32[32]{0:T(128)S(1)}, /*index=5*/f32[...) fusion(f32[32,1]{0,1:T(1,128)S(1)} %get-tuple-element.48, f32[]{:T(128)} %bitcast.2, ...), kind=kLoop, calls=%fused_computation.82 | loop fusion | flops 480 | bytes 1448 | tf_op jit(solution)/shard_map/cond/branch_1_fun/add | solution.py:100
  301.1 11.2 %add_reduce_fusion.4 = (f32[384]{0:T(512)S(1)}, f32[384]{0:T(512)S(1)}, f32[384]{0:T(512)S(1)}, f32[384]{0:T(512)S(1)}, f32[384]{0:T(512)S(1)}, /*index=5*/f32[3...) fusion(f32[1,384]{1,0:T(1,128)S(1)} %get-tuple-element.47, ...), kind=kLoop, calls=%fused_computation.67 | loop fusion | flops 8448 | bytes 21576 | tf_op jit(solution)/shard_map/cond/branch_1_fun/add | solution.py:100
  315.9 2.4 collective-permute-start.8
  319.0 4.1 %collective-permute-done.8 = f32[32,10]{1,0:T(8,128)S(1)} collective-permute-done((f32[32,10]{1,0:T(8,128)S(1)}, f32[32,10]{1,0:T(8,128)S(1)}, u32[]{:S(2)}, u32[]{:S(2)}) %collective-permute-start.8) | collective-permute-done | bytes 1312 | tf_op jit(solution)/shard_map/ppermute | solution.py:15
  323.1 13.3 %fusion.119 = f32[32,384]{1,0:T(8,128)S(1)} fusion(f32[32,384]{1,0:T(8,128)S(1)} %add_divide_fusion, f32[32,10]{1,0:T(8,128)S(1)} %collective-permute-done.9, f32[32,10]{1,0:T(8,128)S(1)} %collective-permute-done.8, f32[]{:T(128)} %bitcast.348, f32[]{:T(128)} %bitcast.347, f32[]{:T(128)} %bitcast.346, f32[]{:T(128)} %bitcast.345, f32[]{:T(128)} %bitcast.344, ...), kind=kLoop, calls=%fused_computation.427 | loop fusion | flops 749568 | bytes 100948 | tf_op jit(solution)/shard_map/add | solution.py:122
  338.3 3.9 %collective-permute-start.10 = (f32[10,384]{1,0:T(8,128)S(1)}, f32[10,384]{1,0:T(8,128)S(1)}, u32[]{:S(2)}, u32[]{:S(2)}) collective-permute-start(f32[10,384]{1,0:T(8,128)S(1)} %get-tuple-element.335), channel_id=1, source_target_pairs={{0,1},{1,2},{2,3},{3,4},{4,5},{5,6},{6,7},{7,8},{8,9},{9,10},{10,1... | collective-permute-start | bytes 46088 | tf_op jit(solution)/shard_map/ppermute | solution.py:15
  342.3 7.8 %collective-permute-done.10 = f32[10,384]{1,0:T(8,128)S(1)} collective-permute-done((f32[10,384]{1,0:T(8,128)S(1)}, f32[10,384]{1,0:T(8,128)S(1)}, u32[]{:S(2)}, u32[]{:S(2)}) %collective-permute-start.10) | collective-permute-done | bytes 15392 | tf_op jit(solution)/shard_map/ppermute | solution.py:15
  350.1 13.6 %fusion.175 = f32[32,384]{1,0:T(8,128)} fusion(f32[32,384]{1,0:T(8,128)S(1)} %fusion.119, f32[10,384]{1,0:T(8,128)S(1)} %collective-permute-done.11, f32[10,384]{1,0:T(8,128)S(1)} %collective-permute-done.10, f32[]{:T(128)} %bitcast.348, f32[]{:T(128)} %bitcast.347, f32[]{:T(128)} %bitcast.346, f32[]{:T(128)} %bitcast.345, f32[]{:T(128)} %bitcast.344, ...), kind=kLoop, calls=%fused_computation.483 | loop fusion | flops 749568 | bytes 129108 | tf_op jit(solution)/shard_map/add | solution.py:126
  (188 shorter events, 38.3 us)
Async XLA Ops:
  0.6 85.6 %copy-start.3 = (f32[21]{0:T(128)S(1)}, f32[21]{0:T(128)}, u32[]{:S(2)}) copy-start(f32[21]{0:T(128)} %param.21) | copy-start | bytes 256
  0.6 120.7 %copy-start.1 = (f32[4,5,6]{2,0,1:T(4,128)S(1)}, f32[4,5,6]{2,0,1:T(4,128)}, u32[]{:S(2)}) copy-start(f32[4,5,6]{2,0,1:T(4,128)} %param.17) | copy-start | bytes 1444
  0.7 120.7 %copy-start = (bf16[5,21,21]{2,1,0:T(8,128)(2,1)S(1)}, bf16[5,21,21]{2,1,0:T(8,128)(2,1)}, u32[]{:S(2)}) copy-start(bf16[5,21,21]{2,1,0:T(8,128)(2,1)} %param.16) | copy-start | bytes 13234
  26.4 21.1 %all-to-all-start = ((bf16[16,32,384]{2,1,0:T(8,128)(2,1)}), bf16[16,32,384]{2,1,0:T(8,128)(2,1)S(1)}, u32[]{:S(2)}, u32[]{:S(2)}) async-start(bf16[16,32,384]{2,1,0:T(8,128)(2,1)} %stack.324), calls=%async_computation | async-start | bytes 786432 | tf_op jit(solution)/shard_map/all_to_all | solution.py:81
  48.3 20.7 %all-to-all-start.1 = ((bf16[16,32,384]{2,1,0:T(8,128)(2,1)}), bf16[16,32,384]{2,1,0:T(8,128)(2,1)S(1)}, u32[]{:S(2)}, u32[]{:S(2)}) async-start(bf16[16,32,384]{2,1,0:T(8,128)(2,1)} %stack.325), calls=%async_computation.1 | async-start | bytes 786432 | tf_op jit(solution)/shard_map/all_to_all | solution.py:81
  69.8 22.5 %all-to-all-start.2 = ((bf16[16,32,384]{2,1,0:T(8,128)(2,1)}), bf16[16,32,384]{2,1,0:T(8,128)(2,1)S(1)}, u32[]{:S(2)}, u32[]{:S(2)}) async-start(bf16[16,32,384]{2,1,0:T(8,128)(2,1)} %stack.326), calls=%async_computation.2 | async-start | bytes 786432 | tf_op jit(solution)/shard_map/all_to_all | solution.py:81
  87.2 19.1 %collective-permute-start.7 = (bf16[52,10]{1,0:T(8,128)(2,1)S(1)}, bf16[52,10]{1,0:T(8,128)(2,1)S(1)}, u32[]{:S(2)}, u32[]{:S(2)}) collective-permute-start(bf16[52,10]{1,0:T(8,128)(2,1)S(1)} %get-tuple-element.349), channel_id=1, source_target_pairs={{16,0},{32,16},{48,32},{64,48},{80,64},{96,80},{112,96},{128,112},... | collective-permute-start | bytes 3128 | tf_op jit(solution)/shard_map/ppermute | solution.py:16
  90.4 17.9 %collective-permute-start.6 = (bf16[52,10]{1,0:T(8,128)(2,1)S(1)}, bf16[52,10]{1,0:T(8,128)(2,1)S(1)}, u32[]{:S(2)}, u32[]{:S(2)}) collective-permute-start(bf16[52,10]{1,0:T(8,128)(2,1)S(1)} %get-tuple-element.348), channel_id=1, source_target_pairs={{0,16},{16,32},{32,48},{48,64},{64,80},{80,96},{96,112},{112,128},... | collective-permute-start | bytes 3128 | tf_op jit(solution)/shard_map/ppermute | solution.py:15
  92.7 21.4 %collective-permute-start.5 = (bf16[52,10]{1,0:T(8,128)(2,1)S(1)}, bf16[52,10]{1,0:T(8,128)(2,1)S(1)}, u32[]{:S(2)}, u32[]{:S(2)}) collective-permute-start(bf16[52,10]{1,0:T(8,128)(2,1)S(1)} %get-tuple-element.347), channel_id=1, source_target_pairs={{16,0},{32,16},{48,32},{64,48},{80,64},{96,80},{112,96},{128,112},... | collective-permute-start | bytes 3128 | tf_op jit(solution)/shard_map/ppermute | solution.py:16
  98.5 17.6 %collective-permute-start.4 = (bf16[52,10]{1,0:T(8,128)(2,1)S(1)}, bf16[52,10]{1,0:T(8,128)(2,1)S(1)}, u32[]{:S(2)}, u32[]{:S(2)}) collective-permute-start(bf16[52,10]{1,0:T(8,128)(2,1)S(1)} %get-tuple-element.346), channel_id=1, source_target_pairs={{0,16},{16,32},{32,48},{48,64},{64,80},{80,96},{96,112},{112,128},... | collective-permute-start | bytes 3128 | tf_op jit(solution)/shard_map/ppermute | solution.py:15
  100.5 15.7 %collective-permute-start.3 = (bf16[52,10]{1,0:T(8,128)(2,1)S(1)}, bf16[52,10]{1,0:T(8,128)(2,1)S(1)}, u32[]{:S(2)}, u32[]{:S(2)}) collective-permute-start(bf16[52,10]{1,0:T(8,128)(2,1)S(1)} %get-tuple-element.345), channel_id=1, source_target_pairs={{16,0},{32,16},{48,32},{64,48},{80,64},{96,80},{112,96},{128,112},... | collective-permute-start | bytes 3128 | tf_op jit(solution)/shard_map/ppermute | solution.py:16
  106.3 9.8 %collective-permute-start.2 = (bf16[52,10]{1,0:T(8,128)(2,1)S(1)}, bf16[52,10]{1,0:T(8,128)(2,1)S(1)}, u32[]{:S(2)}, u32[]{:S(2)}) collective-permute-start(bf16[52,10]{1,0:T(8,128)(2,1)S(1)} %get-tuple-element.344), channel_id=1, source_target_pairs={{0,16},{16,32},{32,48},{48,64},{64,80},{80,96},{96,112},{112,128},... | collective-permute-start | bytes 3128 | tf_op jit(solution)/shard_map/ppermute | solution.py:15
  108.2 8.0 %collective-permute-start.1 = (bf16[52,10]{1,0:T(8,128)(2,1)S(1)}, bf16[52,10]{1,0:T(8,128)(2,1)S(1)}, u32[]{:S(2)}, u32[]{:S(2)}) collective-permute-start(bf16[52,10]{1,0:T(8,128)(2,1)S(1)} %get-tuple-element.340), channel_id=1, source_target_pairs={{16,0},{32,16},{48,32},{64,48},{80,64},{96,80},{112,96},{128,112},... | collective-permute-start | bytes 3128 | tf_op jit(solution)/shard_map/ppermute | solution.py:16
  114.1 7.1 %collective-permute-start = (bf16[52,10]{1,0:T(8,128)(2,1)S(1)}, bf16[52,10]{1,0:T(8,128)(2,1)S(1)}, u32[]{:S(2)}, u32[]{:S(2)}) collective-permute-start(bf16[52,10]{1,0:T(8,128)(2,1)S(1)} %get-tuple-element.339), channel_id=1, source_target_pairs={{0,16},{16,32},{32,48},{48,64},{64,80},{80,96},{96,112},{112,128},... | collective-permute-start | bytes 3128 | tf_op jit(solution)/shard_map/ppermute | solution.py:15
  313.9 49.8 %copy-start.2 = (f32[32,384]{1,0:T(8,128)}, f32[32,384]{1,0:T(8,128)S(1)}, u32[]{:S(2)}) copy-start(f32[32,384]{1,0:T(8,128)S(1)} %add_divide_fusion) | copy-start | bytes 147460
  314.0 5.0 %collective-permute-start.9 = (f32[32,10]{1,0:T(8,128)S(1)}, f32[32,10]{1,0:T(8,128)S(1)}, u32[]{:S(2)}, u32[]{:S(2)}) collective-permute-start(f32[32,10]{1,0:T(8,128)S(1)} %get-tuple-element.338), channel_id=1, source_target_pairs={{16,0},{32,16},{48,32},{64,48},{80,64},{96,80},{112,96},{128,112},... | collective-permute-start | bytes 3848 | tf_op jit(solution)/shard_map/ppermute | solution.py:16
  315.9 7.2 %collective-permute-start.8 = (f32[32,10]{1,0:T(8,128)S(1)}, f32[32,10]{1,0:T(8,128)S(1)}, u32[]{:S(2)}, u32[]{:S(2)}) collective-permute-start(f32[32,10]{1,0:T(8,128)S(1)} %get-tuple-element.337), channel_id=1, source_target_pairs={{0,16},{16,32},{32,48},{48,64},{64,80},{80,96},{96,112},{112,128},... | collective-permute-start | bytes 3848 | tf_op jit(solution)/shard_map/ppermute | solution.py:15
  336.4 5.9 %collective-permute-start.11 = (f32[10,384]{1,0:T(8,128)S(1)}, f32[10,384]{1,0:T(8,128)S(1)}, u32[]{:S(2)}, u32[]{:S(2)}) collective-permute-start(f32[10,384]{1,0:T(8,128)S(1)} %get-tuple-element.336), channel_id=1, source_target_pairs={{1,0},{2,1},{3,2},{4,3},{5,4},{6,5},{7,6},{8,7},{9,8},{10,9},{11,1... | collective-permute-start | bytes 46088 | tf_op jit(solution)/shard_map/ppermute | solution.py:16
  338.3 11.7 %collective-permute-start.10 = (f32[10,384]{1,0:T(8,128)S(1)}, f32[10,384]{1,0:T(8,128)S(1)}, u32[]{:S(2)}, u32[]{:S(2)}) collective-permute-start(f32[10,384]{1,0:T(8,128)S(1)} %get-tuple-element.335), channel_id=1, source_target_pairs={{0,1},{1,2},{2,3},{3,4},{4,5},{5,6},{6,7},{7,8},{8,9},{9,10},{10,1... | collective-permute-start | bytes 46088 | tf_op jit(solution)/shard_map/ppermute | solution.py:15
